TPU v7x, 128 devices: a whole 4x4x4 slice. The times are simulated.
128 devices in a mesh: tok: 8 (over x, core), voc: 16 (over z, y).
Axes of the slice: x: 4, y: 4, z: 4, core: 2. Of those that a mesh axis runs over, the one named last changes fastest.
Arguments:
- hidden: bfloat16 [256, 32, 2048], P(('tok', 'voc')), may hold values from -40 to 40
- norm_gain: float32 [2048], replicated, may hold values from 0.5 to 1.5
- head_weight: bfloat16 [2048, 102400], P(None, 'voc'), may hold values from -2 to 2
- lengths: int32 [256], P(('tok', 'voc')), may hold values from 12 to 24, as said below
- offsets: int32 [256], P(('tok', 'voc')), may hold values from 0 to 8
- slot_request: int32 [256], replicated, may hold values from 0 to 255, each once
- targets: int32 [256, 32], P(('tok', 'voc')), may hold values from 0 to 102399
Outputs:
- token_logprob: float32 [256, 32], P(('tok', 'voc'))
- token_entropy: float32 [256, 32], P(('tok', 'voc'))
Inputs may be any that keep to these rules, and one draw needn't show every extreme that they name: `lengths`: each request has 12 to 24 response rows; all 2 requests of some one scoring device have exactly 24. Response rows end within the window: offsets + lengths <= 32. `slot_request`: every request appears in exactly one slot.
All inputs are finite; a program needn't handle non-finite values.
Results may differ from a plain program's by a relative error of at most 0.00145.
Values may be sent and summed in bfloat16 or wider, within the bound.
A program may use at most 128 MiB of HBM per device.

v0:
```python
import jax
import jax.numpy as jnp
from jax import lax
from jax.sharding import PartitionSpec as P

EPS = 1e-06


def normalize(hidden, norm_gain):
    values = hidden.astype(jnp.float32)
    square = jnp.mean(values * values, axis=-1, keepdims=True)
    return (values * lax.rsqrt(square + EPS) * norm_gain).astype(jnp.bfloat16)


def shards(hidden, norm_gain, head_weight, lengths, offsets, slot_request, targets):
    req_dev, span, width = hidden.shape
    vocab_dev = head_weight.shape[1]
    normed = normalize(hidden, norm_gain).reshape(req_dev * span, width)
    position = jnp.arange(span, dtype=jnp.int32)[None, :]
    in_span = (
        (position >= offsets[:, None]) & (position < offsets[:, None] + lengths[:, None])
    ).reshape(-1)
    flat_targets = targets.reshape(-1)
    own_count = normed.shape[0]
    group_matrix, group_targets = (
        lax.all_gather(normed, "voc", axis=0, tiled=True),
        lax.all_gather(flat_targets, "voc", axis=0, tiled=True),
    )
    logits = jnp.dot(group_matrix, head_weight, preferred_element_type=jnp.float32)
    shard_index = lax.axis_index("voc")
    local_column = group_targets - shard_index * vocab_dev
    target_hit = jnp.arange(vocab_dev, dtype=jnp.int32)[None, :] == local_column[:, None]
    picked = jnp.sum(jnp.where(target_hit, logits, 0.0), axis=1)
    row_peak = jnp.max(logits, axis=1)
    scaled = jnp.exp(logits - row_peak[:, None])
    exp_sum = jnp.sum(scaled, axis=1)
    exp_dot = jnp.sum(scaled * logits, axis=1)
    first_row = shard_index * own_count
    peak_all = lax.pmax(row_peak, "voc")
    rescale = jnp.exp(row_peak - peak_all)
    sum_all, dot_all, pick_all = lax.psum((exp_sum * rescale, exp_dot * rescale, picked), "voc")
    peak_own = lax.dynamic_slice_in_dim(peak_all, first_row, own_count)
    sum_own = lax.dynamic_slice_in_dim(sum_all, first_row, own_count)
    dot_own = lax.dynamic_slice_in_dim(dot_all, first_row, own_count)
    pick_own = lax.dynamic_slice_in_dim(pick_all, first_row, own_count)
    log_total = jnp.log(sum_own)
    logprob = pick_own - peak_own - log_total
    entropy = peak_own + log_total - dot_own / sum_own
    logprob_rows = jnp.where(in_span, logprob, 0.0).reshape(req_dev, span)
    entropy_rows = jnp.where(in_span, entropy, 0.0).reshape(req_dev, span)
    device = lax.axis_index(("tok", "voc"))
    every_logprob, every_entropy = (
        lax.all_gather(logprob_rows, ("tok", "voc"), axis=0, tiled=True),
        lax.all_gather(entropy_rows, ("tok", "voc"), axis=0, tiled=True),
    )
    wanted = device * req_dev + jnp.arange(req_dev, dtype=jnp.int32)
    picking = slot_request[None, :] == wanted[:, None]
    token_logprob = jnp.sum(jnp.where(picking[:, :, None], every_logprob[None, :, :], 0.0), axis=1)
    token_entropy = jnp.sum(jnp.where(picking[:, :, None], every_entropy[None, :, :], 0.0), axis=1)
    return (token_logprob, token_entropy)


def solution(mesh):
    placed = (
        P(("tok", "voc"), None, None),
        P(),
        P(None, "voc"),
        P(("tok", "voc")),
        P(("tok", "voc")),
        P(),
        P(("tok", "voc"), None),
    )
    return jax.shard_map(
        shards,
        mesh=mesh,
        in_specs=placed,
        out_specs=(P(("tok", "voc"), None), P(("tok", "voc"), None)),
        check_vma=False,
    )
```

profile of v0, /device:TPU:0, one launch (start us, length us, event | category | flops | bytes accessed | tf_op | source)
XLA Modules:
  0.0 326.7 jit_solution(2216714420504681096)
XLA Ops:
  7.2 0.0 all-gather.4.cloned.1.call-start
  7.2 1.1 fusion.1
  8.3 1.8 fusion.3
  10.1 0.0 all-gather.4.cloned.1.call-update
  10.1 0.7 add.46
  10.8 0.7 compare_and_fusion
  11.5 0.1 and.10
  11.6 0.8 reshape.74
  12.4 1.2 dynamic-slice
  14.3 0.2 dynamic-update-slice
  14.5 17.9 %all-reduce = s32[1024]{0:T(1024)S(1)} all-reduce(s32[1024]{0:T(1024)S(1)} %dynamic-update-slice), channel_id=1, replica_groups=mesh['tok'=8,'voc'=16] {'voc'}, use_global_device_ids=true, to_apply=%add | all-reduce | flops 1024 | bytes 8192
  32.4 0.8 broadcast_compare_fusion
  33.2 31.1 %all-gather.4.cloned.1.call-done = bf16[1024,2048]{1,0:T(8,128)(2,1)} async-done(((bf16[64,2048]{1,0:T(8,128)(2,1)}), bf16[1024,2048]{1,0:T(8,128)(2,1)}) %all-gather.4.cloned.1.call-update) | async-done | bytes 4194320 | tf_op jit(solution)/shard_map/all_gather | solution.py:26
  64.3 34.9 %fusion.6 = (f32[1024]{0:T(1024)S(1)}, f32[1024,6400]{1,0:T(8,128)}) fusion(bf16[1024,2048]{1,0:T(8,128)(2,1)} %all-gather.4.cloned.1.call-done, bf16[2048,6400]{1,0:T(8,128)(2,1)} %param.9), kind=kOutput, calls=%fused_computation.22 | convolution fusion | flops 26850099200 | bytes 56627200 | tf_op jit(solution)/shard_map/dot_general | solution.py:29
  99.2 38.5 %pmax.7 = f32[1024]{0:T(1024)S(1)} all-reduce(f32[1024]{0:T(1024)S(1)} %get-tuple-element.14), channel_id=1, replica_groups=mesh['tok'=8,'voc'=16] {'voc'}, use_global_device_ids=true, to_apply=%region_4.5 | all-reduce | flops 1024 | bytes 8192 | tf_op jit(solution)/shard_map/pmax | solution.py:39
  137.7 11.4 %multiply_reduce_fusion = (f32[1024]{0:T(1024)S(1)}, f32[1024]{0:T(1024)S(1)}, f32[1024]{0:T(1024)S(1)}) fusion(f32[1024,6400]{1,0:T(8,128)} %get-tuple-element.15, f32[1024]{0:T(1024)S(1)} %get-tuple-element.14, s32[1024]{0:T(1024)S(1)} %broadcast_subtract_fusion), kind=kLoop, calls=%fused_computation | loop fusion | flops 45872128 | bytes 26234880 | tf_op jit(solution)/shard_map/reduce_sum | solution.py:37
  149.1 69.6 %all-reduce.1 = (f32[1024]{0:T(1024)S(1)}, f32[1024]{0:T(1024)S(1)}, f32[1024]{0:T(1024)S(1)}) all-reduce(f32[1024]{0:T(1024)S(1)} %get-tuple-element.13, f32[1024]{0:T(1024)S(1)} %get-tuple-element.12, f32[1024]{0:T(1024)S(1)} %get-tuple-element.4), channel_id=1, replica_groups=mesh['tok'=8,'voc'=16] {'voc'}, use_global_device_ids=true, to_apply=%region_9.10 | all-reduce | flops 3072 | bytes 24576 | tf_op jit(solution)/shard_map/psum | solution.py:41
  218.7 0.1 subtract_select_fusion.1
  218.8 0.1 reshape.79
  218.9 49.9 %all-gather.1 = f32[128,2,32]{2,1,0:T(2,128)S(1)} all-gather(f32[1,2,32]{2,1,0:T(2,128)S(1)} %reshape.79), channel_id=1, replica_groups=mesh['tok'=8,'voc'=16] {'tok','voc'}, dimensions={0}, use_global_device_ids=true | all-gather | bytes 33024 | tf_op jit(solution)/shard_map/all_gather | solution.py:54
  268.8 0.1 copy.10
  268.8 0.1 reshape.77
  268.9 50.2 %all-gather = f32[128,2,32]{2,1,0:T(2,128)S(1)} all-gather(f32[1,2,32]{2,1,0:T(2,128)S(1)} %reshape.77), channel_id=1, replica_groups=mesh['tok'=8,'voc'=16] {'tok','voc'}, dimensions={0}, use_global_device_ids=true | all-gather | bytes 33024 | tf_op jit(solution)/shard_map/all_gather | solution.py:53
  319.1 0.1 copy.9
  319.2 0.7 select_reduce_fusion.1
  (5 shorter events, 0.0 us)
Async XLA Ops:
  7.2 57.1 %all-gather.4.cloned.1.call-start = ((), (), s32[]{:S(2)}) async-start(), calls=%async_computation | async-start | bytes 4456448 | tf_op jit(solution)/shard_map/all_gather | solution.py:26
Sparse Core Ops, SparseCore 0:
  10.2 53.9 all-gather.3
where the time goes:
time: 327 us
  blocking collectives  226 us (69%)
  matrix products  34.9 us (11%)
  waiting for transfers between devices  31.1 us (10%)
  other arithmetic  17.2 us (5%)
  between operations  14.7 us (4%)
    psum x1, blocking collectives, shards(): lax.psum((exp_sum * rescale, exp_dot * rescale, picked), 'voc')  69.6 us
    all_gather x1, blocking collectives, shards(): lax.all_gather(logprob_rows, ('tok', 'voc'), axis=0, tiled=True)  50.2 us
    all_gather x1, blocking collectives, shards(): lax.all_gather(entropy_rows, ('tok', 'voc'), axis=0, tiled=True)  49.9 us
    pmax x1, blocking collectives, shards(): peak_all = lax.pmax(row_peak, 'voc')  38.5 us
    dot_general x1, matrix products, shards(): jnp.dot(group_matrix, head_weight, preferred_element_type=jnp.float32)  34.9 us
    all_gather x1, waiting for transfers between devices, shards(): lax.all_gather(normed, 'voc', axis=0, tiled=True)  31.1 us
    unnamed x1, blocking collectives  17.9 us
    reduce_sum x1, other arithmetic, shards(): exp_dot = jnp.sum(scaled * logits, axis=1)  11.4 us
  transfers between devices with their start and end apart: 1, of which 1 were waited for; matrix products, arithmetic and copies ran while one was open for 1% of the time, Pallas kernels for 0%

commit v1 on v0

--- a/solution.py
+++ b/solution.py
@@ -22,8 +22,35 @@
     ).reshape(-1)
     flat_targets = targets.reshape(-1)
     own_count = normed.shape[0]
+
+    def update_pools_now(inp, axis_no):
+        b_now = lax.psum(1, "voc")
+        piece_next = lax.axis_index("voc")
+        state_next, v1, top = (b_now, piece_next, inp.shape[axis_no])
+        all_blocks = tuple(((hop_no, (hop_no + 1) % state_next) for hop_no in range(state_next)))
+        series = tuple(((hop_no, (hop_no - 1) % state_next) for hop_no in range(state_next)))
+        ready = jnp.zeros(
+            (*inp.shape[:axis_no], state_next * top, *inp.shape[axis_no + 1 :]), inp.dtype
+        )
+        ready = lax.dynamic_update_slice_in_dim(ready, inp, v1 * top, axis=axis_no)
+        small = x_new = inp
+        after = state_next // 2
+        d = 1
+        while d < after + 1:
+            small = lax.ppermute(small, "voc", all_blocks)
+            ready = lax.dynamic_update_slice_in_dim(
+                ready, small, (v1 - d) % state_next * top, axis=axis_no
+            )
+            if d < state_next - after:
+                x_new = lax.ppermute(x_new, "voc", series)
+                ready = lax.dynamic_update_slice_in_dim(
+                    ready, x_new, (v1 + d) % state_next * top, axis=axis_no
+                )
+            d += 1
+        return ready
+
     group_matrix, group_targets = (
-        lax.all_gather(normed, "voc", axis=0, tiled=True),
+        update_pools_now(normed, 0),
         lax.all_gather(flat_targets, "voc", axis=0, tiled=True),
     )
     logits = jnp.dot(group_matrix, head_weight, preferred_element_type=jnp.float32)

time: 327 us -> 358 us (1.095)
  starting transfers between devices: 0.04 us -> 40.6 us
  between operations: 14.7 us -> 1.45 us
  waiting for transfers between devices: 31.1 us -> 41.2 us
  blocking collectives: 226 us -> 220 us
    ppermute x0 -> x15, waiting for transfers between devices: none -> 41.2 us  [the longest x8 40.9 us: update_pools_now(): small = lax.ppermute(small, 'voc', all_blocks)]
    ppermute x0 -> x15, starting transfers between devices: none -> 40.6 us  [the longest x7 38 us: update_pools_now(): x_new = lax.ppermute(x_new, 'voc', series)]
    all_gather x1 -> x0, waiting for transfers between devices: 31.1 us -> none  [shards(): lax.all_gather(normed, 'voc', axis=0, tiled=True)]
    unnamed x1, blocking collectives: 17.9 us -> 13.2 us
  transfers between devices with their start and end apart: 1 -> 15, of which waited for: 1 -> 9; matrix products, arithmetic and copies ran while one was open for 1% -> 1% of each run, Pallas kernels for 0% -> 0%
where the time goes in v1:
time: 358 us; the launch traced here: 357 us
  blocking collectives  220 us (61%)
  waiting for transfers between devices  41.2 us (12%)
  starting transfers between devices  40.6 us (11%)
  matrix products  33.7 us (9%)
  other arithmetic  16.8 us (5%)
    psum x1, blocking collectives, shards(): lax.psum((exp_sum * rescale, exp_dot * rescale, picked), 'voc')  71.4 us
    all_gather x1, blocking collectives, shards(): lax.all_gather(logprob_rows, ('tok', 'voc'), axis=0, tiled=True)  50.2 us
    all_gather x1, blocking collectives, shards(): lax.all_gather(entropy_rows, ('tok', 'voc'), axis=0, tiled=True)  49.9 us
    ppermute x8, waiting for transfers between devices, update_pools_now(): small = lax.ppermute(small, 'voc', all_blocks)  40.9 us
    ppermute x7, starting transfers between devices, update_pools_now(): x_new = lax.ppermute(x_new, 'voc', series)  38 us
    pmax x1, blocking collectives, shards(): peak_all = lax.pmax(row_peak, 'voc')  35.4 us
    dot_general x1, matrix products, shards(): jnp.dot(group_matrix, head_weight, preferred_element_type=jnp.float32)  33.7 us
    unnamed x1, blocking collectives  13.2 us
  transfers between devices with their start and end apart: 15, of which 9 were waited for; matrix products, arithmetic and copies ran while one was open for 1% of the time, Pallas kernels for 0%

profile of v1, /device:TPU:0, one launch (start us, length us, event | category | flops | bytes accessed | tf_op | source)
XLA Modules:
  0.0 357.3 jit_solution(1329275289332109252)
XLA Ops:
  0.6 1.1 fusion.1
  1.7 1.1 fusion.3
  2.8 1.8 collective-permute-start
  4.6 5.0 %collective-permute-start.1 = (bf16[64,2048]{1,0:T(8,128)(2,1)S(1)}, bf16[64,2048]{1,0:T(8,128)(2,1)S(1)}, u32[]{:S(2)}, u32[]{:S(2)}) collective-permute-start(bf16[64,2048]{1,0:T(8,128)(2,1)S(1)} %bitcast.7), channel_id=1, source_target_pairs={{0,15},{1,0},{2,1},{3,2},{4,3},{5,4},{6,5},{7,6},{8,7},{9,8},{10,9... | collective-permute-start | bytes 786440 | tf_op jit(solution)/shard_map/ppermute | solution.py:45
  9.6 0.8 reshape.74
  10.3 1.2 dynamic-slice
  12.2 0.2 dynamic-update-slice
  12.5 13.2 %all-reduce = s32[1024]{0:T(1024)S(1)} all-reduce(s32[1024]{0:T(1024)S(1)} %dynamic-update-slice), channel_id=1, replica_groups=mesh['tok'=8,'voc'=16] {'voc'}, use_global_device_ids=true, to_apply=%add | all-reduce | flops 1024 | bytes 8192
  25.7 0.7 add.167
  26.3 0.8 broadcast_compare_fusion
  27.1 0.7 compare_and_fusion
  27.8 0.1 and.71
  27.9 0.5 broadcast_in_dim.57
  28.5 0.0 collective-permute-done
  28.5 0.8 collective-permute-start.2
  29.2 0.0 collective-permute-done.1
  29.3 4.7 %collective-permute-start.3 = (bf16[64,2048]{1,0:T(8,128)(2,1)S(1)}, bf16[64,2048]{1,0:T(8,128)(2,1)S(1)}, u32[]{:S(2)}, u32[]{:S(2)}) collective-permute-start(bf16[64,2048]{1,0:T(8,128)(2,1)S(1)} %collective-permute-done.1), channel_id=1, source_target_pairs={{0,15},{1,0},{2,1},{3,2},{4,3},{5,4},{6,5},{7,6},{8,7},{9,8},{10,9... | collective-permute-start | bytes 786440 | tf_op jit(solution)/shard_map/ppermute | solution.py:45
  34.0 4.3 %collective-permute-done.2 = bf16[64,2048]{1,0:T(8,128)(2,1)S(1)} collective-permute-done((bf16[64,2048]{1,0:T(8,128)(2,1)S(1)}, bf16[64,2048]{1,0:T(8,128)(2,1)S(1)}, u32[]{:S(2)}, u32[]{:S(2)}) %collective-permute-start.2) | collective-permute-done | bytes 262176 | tf_op jit(solution)/shard_map/ppermute | solution.py:40
  38.2 0.0 collective-permute-start.4
  38.3 0.0 collective-permute-done.3
  38.3 5.3 %collective-permute-start.5 = (bf16[64,2048]{1,0:T(8,128)(2,1)S(1)}, bf16[64,2048]{1,0:T(8,128)(2,1)S(1)}, u32[]{:S(2)}, u32[]{:S(2)}) collective-permute-start(bf16[64,2048]{1,0:T(8,128)(2,1)S(1)} %collective-permute-done.3), channel_id=1, source_target_pairs={{0,15},{1,0},{2,1},{3,2},{4,3},{5,4},{6,5},{7,6},{8,7},{9,8},{10,9... | collective-permute-start | bytes 786440 | tf_op jit(solution)/shard_map/ppermute | solution.py:45
  43.7 4.6 %collective-permute-done.4 = bf16[64,2048]{1,0:T(8,128)(2,1)S(1)} collective-permute-done((bf16[64,2048]{1,0:T(8,128)(2,1)S(1)}, bf16[64,2048]{1,0:T(8,128)(2,1)S(1)}, u32[]{:S(2)}, u32[]{:S(2)}) %collective-permute-start.4) | collective-permute-done | bytes 262176 | tf_op jit(solution)/shard_map/ppermute | solution.py:40
  48.3 0.0 collective-permute-start.6
  48.3 5.6 %collective-permute-start.7 = (bf16[64,2048]{1,0:T(8,128)(2,1)S(1)}, bf16[64,2048]{1,0:T(8,128)(2,1)S(1)}, u32[]{:S(2)}, u32[]{:S(2)}) collective-permute-start(bf16[64,2048]{1,0:T(8,128)(2,1)S(1)} %collective-permute-done.5), channel_id=1, source_target_pairs={{0,15},{1,0},{2,1},{3,2},{4,3},{5,4},{6,5},{7,6},{8,7},{9,8},{10,9... | collective-permute-start | bytes 786440 | tf_op jit(solution)/shard_map/ppermute | solution.py:45
  54.0 5.5 %collective-permute-done.6 = bf16[64,2048]{1,0:T(8,128)(2,1)S(1)} collective-permute-done((bf16[64,2048]{1,0:T(8,128)(2,1)S(1)}, bf16[64,2048]{1,0:T(8,128)(2,1)S(1)}, u32[]{:S(2)}, u32[]{:S(2)}) %collective-permute-start.6) | collective-permute-done | bytes 262176 | tf_op jit(solution)/shard_map/ppermute | solution.py:40
  59.5 0.1 collective-permute-done.7
  59.6 5.8 %collective-permute-start.9 = (bf16[64,2048]{1,0:T(8,128)(2,1)S(1)}, bf16[64,2048]{1,0:T(8,128)(2,1)S(1)}, u32[]{:S(2)}, u32[]{:S(2)}) collective-permute-start(bf16[64,2048]{1,0:T(8,128)(2,1)S(1)} %collective-permute-done.7), channel_id=1, source_target_pairs={{0,15},{1,0},{2,1},{3,2},{4,3},{5,4},{6,5},{7,6},{8,7},{9,8},{10,9... | collective-permute-start | bytes 786440 | tf_op jit(solution)/shard_map/ppermute | solution.py:45
  65.5 6.4 %collective-permute-done.8 = bf16[64,2048]{1,0:T(8,128)(2,1)S(1)} collective-permute-done((bf16[64,2048]{1,0:T(8,128)(2,1)S(1)}, bf16[64,2048]{1,0:T(8,128)(2,1)S(1)}, u32[]{:S(2)}, u32[]{:S(2)}) %collective-permute-start.8) | collective-permute-done | bytes 262176 | tf_op jit(solution)/shard_map/ppermute | solution.py:40
  71.8 0.2 collective-permute-done.9
  72.0 5.8 %collective-permute-start.11 = (bf16[64,2048]{1,0:T(8,128)(2,1)S(1)}, bf16[64,2048]{1,0:T(8,128)(2,1)S(1)}, u32[]{:S(2)}, u32[]{:S(2)}) collective-permute-start(bf16[64,2048]{1,0:T(8,128)(2,1)S(1)} %collective-permute-done.9), channel_id=1, source_target_pairs={{0,15},{1,0},{2,1},{3,2},{4,3},{5,4},{6,5},{7,6},{8,7},{9,8},{10,9... | collective-permute-start | bytes 786440 | tf_op jit(solution)/shard_map/ppermute | solution.py:45
  77.8 5.6 %collective-permute-done.10 = bf16[64,2048]{1,0:T(8,128)(2,1)S(1)} collective-permute-done((bf16[64,2048]{1,0:T(8,128)(2,1)S(1)}, bf16[64,2048]{1,0:T(8,128)(2,1)S(1)}, u32[]{:S(2)}, u32[]{:S(2)}) %collective-permute-start.10) | collective-permute-done | bytes 262176 | tf_op jit(solution)/shard_map/ppermute | solution.py:40
  83.5 0.0 collective-permute-done.11
  83.5 5.8 %collective-permute-start.13 = (bf16[64,2048]{1,0:T(8,128)(2,1)S(1)}, bf16[64,2048]{1,0:T(8,128)(2,1)S(1)}, u32[]{:S(2)}, u32[]{:S(2)}) collective-permute-start(bf16[64,2048]{1,0:T(8,128)(2,1)S(1)} %collective-permute-done.11), channel_id=1, source_target_pairs={{0,15},{1,0},{2,1},{3,2},{4,3},{5,4},{6,5},{7,6},{8,7},{9,8},{10,9... | collective-permute-start | bytes 786440 | tf_op jit(solution)/shard_map/ppermute | solution.py:45
  89.4 4.9 %collective-permute-done.12 = bf16[64,2048]{1,0:T(8,128)(2,1)S(1)} collective-permute-done((bf16[64,2048]{1,0:T(8,128)(2,1)S(1)}, bf16[64,2048]{1,0:T(8,128)(2,1)S(1)}, u32[]{:S(2)}, u32[]{:S(2)}) %collective-permute-start.12) | collective-permute-done | bytes 262176 | tf_op jit(solution)/shard_map/ppermute | solution.py:40
  94.2 0.0 collective-permute-start.14
  94.3 9.6 %collective-permute-done.14 = bf16[64,2048]{1,0:T(8,128)(2,1)S(1)} collective-permute-done((bf16[64,2048]{1,0:T(8,128)(2,1)S(1)}, bf16[64,2048]{1,0:T(8,128)(2,1)S(1)}, u32[]{:S(2)}, u32[]{:S(2)}) %collective-permute-start.14) | collective-permute-done | bytes 262176 | tf_op jit(solution)/shard_map/ppermute | solution.py:40
  104.0 33.7 %fusion.6 = (f32[1024]{0:T(1024)S(1)}, f32[1024,6400]{1,0:T(8,128)}) fusion(bf16[1024,2048]{1,0:T(8,128)(2,1)S(1)} %constant_dynamic-update-slice_fusion, bf16[2048,6400]{1,0:T(8,128)(2,1)} %param.9), kind=kOutput, calls=%fused_computation.38 | convolution fusion | flops 26850099200 | bytes 56627200 | tf_op jit(solution)/shard_map/dot_general | solution.py:56
  137.7 35.4 %pmax.7 = f32[1024]{0:T(1024)S(1)} all-reduce(f32[1024]{0:T(1024)S(1)} %get-tuple-element.14), channel_id=1, replica_groups=mesh['tok'=8,'voc'=16] {'voc'}, use_global_device_ids=true, to_apply=%region_4.5 | all-reduce | flops 1024 | bytes 8192 | tf_op jit(solution)/shard_map/pmax | solution.py:66
  173.1 11.7 %multiply_reduce_fusion = (f32[1024]{0:T(1024)S(1)}, f32[1024]{0:T(1024)S(1)}, f32[1024]{0:T(1024)S(1)}) fusion(f32[1024,6400]{1,0:T(8,128)} %get-tuple-element.15, f32[1024]{0:T(1024)S(1)} %get-tuple-element.14, s32[1024]{0:T(1024)S(1)} %broadcast_subtract_fusion), kind=kLoop, calls=%fused_computation | loop fusion | flops 45872128 | bytes 26234880 | tf_op jit(solution)/shard_map/reduce_sum | solution.py:64
  184.8 71.4 %all-reduce.1 = (f32[1024]{0:T(1024)S(1)}, f32[1024]{0:T(1024)S(1)}, f32[1024]{0:T(1024)S(1)}) all-reduce(f32[1024]{0:T(1024)S(1)} %get-tuple-element.13, f32[1024]{0:T(1024)S(1)} %get-tuple-element.12, f32[1024]{0:T(1024)S(1)} %get-tuple-element.4), channel_id=1, replica_groups=mesh['tok'=8,'voc'=16] {'voc'}, use_global_device_ids=true, to_apply=%region_9.10 | all-reduce | flops 3072 | bytes 24576 | tf_op jit(solution)/shard_map/psum | solution.py:68
  256.2 0.1 subtract_select_fusion.1
  256.3 0.1 reshape.79
  256.4 49.9 %all-gather.1 = f32[128,2,32]{2,1,0:T(2,128)S(1)} all-gather(f32[1,2,32]{2,1,0:T(2,128)S(1)} %reshape.79), channel_id=1, replica_groups=mesh['tok'=8,'voc'=16] {'tok','voc'}, dimensions={0}, use_global_device_ids=true | all-gather | bytes 33024 | tf_op jit(solution)/shard_map/all_gather | solution.py:81
  306.3 0.1 copy.10
  306.3 0.1 reshape.77
  306.4 50.2 %all-gather = f32[128,2,32]{2,1,0:T(2,128)S(1)} all-gather(f32[1,2,32]{2,1,0:T(2,128)S(1)} %reshape.77), channel_id=1, replica_groups=mesh['tok'=8,'voc'=16] {'tok','voc'}, dimensions={0}, use_global_device_ids=true | all-gather | bytes 33024 | tf_op jit(solution)/shard_map/all_gather | solution.py:80
  356.6 0.1 copy.9
  356.7 0.7 select_reduce_fusion.1
  (26 shorter events, 0.4 us)
Async XLA Ops:
  2.8 25.7 %collective-permute-start = (bf16[64,2048]{1,0:T(8,128)(2,1)S(1)}, bf16[64,2048]{1,0:T(8,128)(2,1)S(1)}, u32[]{:S(2)}, u32[]{:S(2)}) collective-permute-start(bf16[64,2048]{1,0:T(8,128)(2,1)S(1)} %bitcast.6), channel_id=1, source_target_pairs={{0,1},{1,2},{2,3},{3,4},{4,5},{5,6},{6,7},{7,8},{8,9},{9,10},{10,1... | collective-permute-start | bytes 786440 | tf_op jit(solution)/shard_map/ppermute | solution.py:40
  4.6 24.7 %collective-permute-start.1 = (bf16[64,2048]{1,0:T(8,128)(2,1)S(1)}, bf16[64,2048]{1,0:T(8,128)(2,1)S(1)}, u32[]{:S(2)}, u32[]{:S(2)}) collective-permute-start(bf16[64,2048]{1,0:T(8,128)(2,1)S(1)} %bitcast.7), channel_id=1, source_target_pairs={{0,15},{1,0},{2,1},{3,2},{4,3},{5,4},{6,5},{7,6},{8,7},{9,8},{10,9... | collective-permute-start | bytes 786440 | tf_op jit(solution)/shard_map/ppermute | solution.py:45
  28.5 9.8 %collective-permute-start.2 = (bf16[64,2048]{1,0:T(8,128)(2,1)S(1)}, bf16[64,2048]{1,0:T(8,128)(2,1)S(1)}, u32[]{:S(2)}, u32[]{:S(2)}) collective-permute-start(bf16[64,2048]{1,0:T(8,128)(2,1)S(1)} %collective-permute-done), channel_id=1, source_target_pairs={{0,1},{1,2},{2,3},{3,4},{4,5},{5,6},{6,7},{7,8},{8,9},{9,10},{10,1... | collective-permute-start | bytes 786440 | tf_op jit(solution)/shard_map/ppermute | solution.py:40
  29.3 9.0 %collective-permute-start.3 = (bf16[64,2048]{1,0:T(8,128)(2,1)S(1)}, bf16[64,2048]{1,0:T(8,128)(2,1)S(1)}, u32[]{:S(2)}, u32[]{:S(2)}) collective-permute-start(bf16[64,2048]{1,0:T(8,128)(2,1)S(1)} %collective-permute-done.1), channel_id=1, source_target_pairs={{0,15},{1,0},{2,1},{3,2},{4,3},{5,4},{6,5},{7,6},{8,7},{9,8},{10,9... | collective-permute-start | bytes 786440 | tf_op jit(solution)/shard_map/ppermute | solution.py:45
  38.2 10.0 %collective-permute-start.4 = (bf16[64,2048]{1,0:T(8,128)(2,1)S(1)}, bf16[64,2048]{1,0:T(8,128)(2,1)S(1)}, u32[]{:S(2)}, u32[]{:S(2)}) collective-permute-start(bf16[64,2048]{1,0:T(8,128)(2,1)S(1)} %collective-permute-done.2), channel_id=1, source_target_pairs={{0,1},{1,2},{2,3},{3,4},{4,5},{5,6},{6,7},{7,8},{8,9},{9,10},{10,1... | collective-permute-start | bytes 786440 | tf_op jit(solution)/shard_map/ppermute | solution.py:40
  38.3 10.0 %collective-permute-start.5 = (bf16[64,2048]{1,0:T(8,128)(2,1)S(1)}, bf16[64,2048]{1,0:T(8,128)(2,1)S(1)}, u32[]{:S(2)}, u32[]{:S(2)}) collective-permute-start(bf16[64,2048]{1,0:T(8,128)(2,1)S(1)} %collective-permute-done.3), channel_id=1, source_target_pairs={{0,15},{1,0},{2,1},{3,2},{4,3},{5,4},{6,5},{7,6},{8,7},{9,8},{10,9... | collective-permute-start | bytes 786440 | tf_op jit(solution)/shard_map/ppermute | solution.py:45
  48.3 11.2 %collective-permute-start.6 = (bf16[64,2048]{1,0:T(8,128)(2,1)S(1)}, bf16[64,2048]{1,0:T(8,128)(2,1)S(1)}, u32[]{:S(2)}, u32[]{:S(2)}) collective-permute-start(bf16[64,2048]{1,0:T(8,128)(2,1)S(1)} %collective-permute-done.4), channel_id=1, source_target_pairs={{0,1},{1,2},{2,3},{3,4},{4,5},{5,6},{6,7},{7,8},{8,9},{9,10},{10,1... | collective-permute-start | bytes 786440 | tf_op jit(solution)/shard_map/ppermute | solution.py:40
  48.3 11.3 %collective-permute-start.7 = (bf16[64,2048]{1,0:T(8,128)(2,1)S(1)}, bf16[64,2048]{1,0:T(8,128)(2,1)S(1)}, u32[]{:S(2)}, u32[]{:S(2)}) collective-permute-start(bf16[64,2048]{1,0:T(8,128)(2,1)S(1)} %collective-permute-done.5), channel_id=1, source_target_pairs={{0,15},{1,0},{2,1},{3,2},{4,3},{5,4},{6,5},{7,6},{8,7},{9,8},{10,9... | collective-permute-start | bytes 786440 | tf_op jit(solution)/shard_map/ppermute | solution.py:45
  59.5 12.3 %collective-permute-start.8 = (bf16[64,2048]{1,0:T(8,128)(2,1)S(1)}, bf16[64,2048]{1,0:T(8,128)(2,1)S(1)}, u32[]{:S(2)}, u32[]{:S(2)}) collective-permute-start(bf16[64,2048]{1,0:T(8,128)(2,1)S(1)} %collective-permute-done.6), channel_id=1, source_target_pairs={{0,1},{1,2},{2,3},{3,4},{4,5},{5,6},{6,7},{7,8},{8,9},{9,10},{10,1... | collective-permute-start | bytes 786440 | tf_op jit(solution)/shard_map/ppermute | solution.py:40
  59.6 12.4 %collective-permute-start.9 = (bf16[64,2048]{1,0:T(8,128)(2,1)S(1)}, bf16[64,2048]{1,0:T(8,128)(2,1)S(1)}, u32[]{:S(2)}, u32[]{:S(2)}) collective-permute-start(bf16[64,2048]{1,0:T(8,128)(2,1)S(1)} %collective-permute-done.7), channel_id=1, source_target_pairs={{0,15},{1,0},{2,1},{3,2},{4,3},{5,4},{6,5},{7,6},{8,7},{9,8},{10,9... | collective-permute-start | bytes 786440 | tf_op jit(solution)/shard_map/ppermute | solution.py:45
  71.8 11.6 %collective-permute-start.10 = (bf16[64,2048]{1,0:T(8,128)(2,1)S(1)}, bf16[64,2048]{1,0:T(8,128)(2,1)S(1)}, u32[]{:S(2)}, u32[]{:S(2)}) collective-permute-start(bf16[64,2048]{1,0:T(8,128)(2,1)S(1)} %collective-permute-done.8), channel_id=1, source_target_pairs={{0,1},{1,2},{2,3},{3,4},{4,5},{5,6},{6,7},{7,8},{8,9},{9,10},{10,1... | collective-permute-start | bytes 786440 | tf_op jit(solution)/shard_map/ppermute | solution.py:40
  72.0 11.5 %collective-permute-start.11 = (bf16[64,2048]{1,0:T(8,128)(2,1)S(1)}, bf16[64,2048]{1,0:T(8,128)(2,1)S(1)}, u32[]{:S(2)}, u32[]{:S(2)}) collective-permute-start(bf16[64,2048]{1,0:T(8,128)(2,1)S(1)} %collective-permute-done.9), channel_id=1, source_target_pairs={{0,15},{1,0},{2,1},{3,2},{4,3},{5,4},{6,5},{7,6},{8,7},{9,8},{10,9... | collective-permute-start | bytes 786440 | tf_op jit(solution)/shard_map/ppermute | solution.py:45
  83.5 10.8 %collective-permute-start.12 = (bf16[64,2048]{1,0:T(8,128)(2,1)S(1)}, bf16[64,2048]{1,0:T(8,128)(2,1)S(1)}, u32[]{:S(2)}, u32[]{:S(2)}) collective-permute-start(bf16[64,2048]{1,0:T(8,128)(2,1)S(1)} %collective-permute-done.10), channel_id=1, source_target_pairs={{0,1},{1,2},{2,3},{3,4},{4,5},{5,6},{6,7},{7,8},{8,9},{9,10},{10,1... | collective-permute-start | bytes 786440 | tf_op jit(solution)/shard_map/ppermute | solution.py:40
  83.5 10.8 %collective-permute-start.13 = (bf16[64,2048]{1,0:T(8,128)(2,1)S(1)}, bf16[64,2048]{1,0:T(8,128)(2,1)S(1)}, u32[]{:S(2)}, u32[]{:S(2)}) collective-permute-start(bf16[64,2048]{1,0:T(8,128)(2,1)S(1)} %collective-permute-done.11), channel_id=1, source_target_pairs={{0,15},{1,0},{2,1},{3,2},{4,3},{5,4},{6,5},{7,6},{8,7},{9,8},{10,9... | collective-permute-start | bytes 786440 | tf_op jit(solution)/shard_map/ppermute | solution.py:45
  94.2 9.7 %collective-permute-start.14 = (bf16[64,2048]{1,0:T(8,128)(2,1)S(1)}, bf16[64,2048]{1,0:T(8,128)(2,1)S(1)}, u32[]{:S(2)}, u32[]{:S(2)}) collective-permute-start(bf16[64,2048]{1,0:T(8,128)(2,1)S(1)} %collective-permute-done.12), channel_id=1, source_target_pairs={{0,1},{1,2},{2,3},{3,4},{4,5},{5,6},{6,7},{7,8},{8,9},{9,10},{10,1... | collective-permute-start | bytes 786440 | tf_op jit(solution)/shard_map/ppermute | solution.py:40
